TPU v7x, 32 devices: a whole 2x2x4 slice. The times are simulated.
32 devices in a mesh: groups: 2 (over y), snd: 4 (over z), win: 2 (over x), pt: 2 (over core).
Axes of the slice: x: 2, y: 2, z: 4, core: 2. Of those that a mesh axis runs over, the one named last changes fastest.
Arguments:
- flux_state: float32 [4, 256, 16, 128], P(('groups', 'win'), 'snd', 'pt'), parts along dimension 0, may hold values from -6 to 6
- prior_precision: float32 [4, 256, 128], P(('groups', 'win'), 'snd'), parts along dimension 0, may hold values from 0.05 to 0.5
- footprint: bfloat16 [64, 32, 128, 128], P(('groups', 'snd'), 'win'), parts along dimension 0, may hold values from -0.125 to 0.125
- tile_ids: int32 [64, 32], P(('groups', 'snd'), 'win'), parts along dimension 0, may hold values from 0 to 255, as said below
- observed: float32 [64, 128], P(('groups', 'snd')), parts along dimension 0, may hold values from -6 to 6
- obs_weight: float32 [64, 128], P(('groups', 'snd')), parts along dimension 0, may hold values from 0.1 to 1
Outputs:
- gradient: float32 [4, 256, 16, 128], P(('groups', 'win'), 'snd', 'pt'), parts along dimension 0
There are 2 independent parts, one for each index of `groups`. A program takes and returns all parts, laid end to end along the dimension named above; each array names one. Nothing has to cross between parts.
Inputs may be any that keep to these rules, and one draw needn't show every extreme that they name: `tile_ids`: column block w (entries w * 16 to w * 16 + 15) belongs to window w. Within the 8 rows and 16 columns of one window held by one device the entries are distinct, and at most 64 of them lie among the 64 tiles t with the same t // 64; in every window one such range is named exactly 64 times by every device.
All inputs are finite; a program needn't handle non-finite values.
Results may differ from a plain program's by a relative error of at most 0.0029.
Values may be sent and summed in bfloat16 or wider, within the bound.
No kernel may reach another device: no remote copies, remote signals or barrier semaphores. Data moves between devices by JAX's collectives and lax.ppermute only.
A program may use at most 64 MiB of HBM per device.

v0:
```python
import jax
import jax.numpy as jnp
from jax import lax
from jax.sharding import PartitionSpec as P


def body(flux_state, prior_precision, footprint, tile_ids, observed, obs_weight):
    flux_local = flux_state[0]
    own_tiles, half_points, tile_cells = flux_local.shape
    blocks, tile_depth = tile_ids.shape
    ref_count = blocks * tile_depth
    flat_ids = tile_ids.reshape(ref_count)
    rounded = flux_local.astype(jnp.bfloat16)
    window_flux = lax.all_gather(rounded, "snd", axis=0, tiled=True)
    gathered = window_flux[flat_ids].reshape(blocks, tile_depth, half_points, tile_cells)
    window_part = jnp.einsum(
        "bksf,bkpf->bps", footprint, gathered, preferred_element_type=jnp.float32
    )
    modeled = lax.psum(window_part, "win")
    residual = (obs_weight[:, None, :] * (modeled - observed[:, None, :])).astype(jnp.bfloat16)
    contrib = jnp.einsum("bps,bksf->bkpf", residual, footprint, preferred_element_type=jnp.float32)
    contrib = contrib.reshape(ref_count, half_points * tile_cells)
    window_tiles = window_flux.shape[0]
    dense_terms = (
        jnp.zeros((window_tiles, half_points * tile_cells), jnp.float32).at[flat_ids].add(contrib)
    )
    summed = lax.psum_scatter(
        dense_terms.reshape(own_tiles * lax.axis_size("snd"), half_points, tile_cells),
        "snd",
        scatter_dimension=0,
        tiled=True,
    )
    gradient = summed + prior_precision[0][:, None, :] * flux_local
    return gradient[None]


def solution(mesh):
    placed = (
        P(("groups", "win"), "snd", "pt", None),
        P(("groups", "win"), "snd", None),
        P(("groups", "snd"), "win", None, None),
        P(("groups", "snd"), "win"),
        P(("groups", "snd"), None),
        P(("groups", "snd"), None),
    )
    return jax.shard_map(
        body,
        mesh=mesh,
        in_specs=placed,
        out_specs=P(("groups", "win"), "snd", "pt", None),
        check_vma=False,
    )
```

profile of v0, /device:TPU:0, one launch (start us, length us, event | category | flops | bytes accessed | tf_op | source)
XLA Modules:
  0.0 80.9 jit_solution(8460589797217001848)
XLA Ops:
  6.5 0.0 copy-start.3
  6.5 0.0 copy-start.2
  6.5 0.0 reduce-scatter.2.cloned.1.call-start
  6.5 0.8 reshape.43
  7.3 1.0 %bitcast_convert_fusion = bf16[64,8,128]{2,1,0:T(8,128)(2,1)S(1)} fusion(f32[1,64,8,128]{3,2,1,0:T(8,128)} %param.6), kind=kLoop, calls=%fused_computation.8 | loop fusion | flops 65536 | bytes 393216 | tf_op jit(solution)/shard_map/convert_element_type | solution.py:13
  8.3 17.4 %all_gather.3 = bf16[256,8,128]{2,1,0:T(8,128)(2,1)S(1)} all-gather(bf16[64,8,128]{2,1,0:T(8,128)(2,1)S(1)} %bitcast_convert_fusion), channel_id=1, replica_groups=mesh['groups'=2,'snd'=4,'win'=2,'pt'=2] {'snd'}, dimensions={0}, use_global_device_ids=true | all-gather | bytes 655360 | tf_op jit(solution)/shard_map/all_gather | solution.py:14
  25.7 0.7 gather_fusion
  26.4 3.4 %convolution_bitcast_fusion = f32[8,8,128]{2,1,0:T(8,128)S(1)} fusion(bf16[8,16,8,128]{3,2,1,0:T(8,128)(2,1)S(1)} %bitcast.35, bf16[8,16,128,128]{3,2,1,0:T(8,128)(2,1)} %param.8), kind=kOutput, calls=%fused_computation.2 | convolution fusion | flops 33554432 | bytes 4489216 | tf_op jit(solution)/shard_map/bksf,bkpf->bps/dot_general | solution.py:16
  29.7 8.4 %psum.7 = f32[8,8,128]{2,1,0:T(8,128)S(1)} all-reduce(f32[8,8,128]{2,1,0:T(8,128)S(1)} %convolution_bitcast_fusion), channel_id=1, replica_groups=mesh['groups'=2,'snd'=4,'win'=2,'pt'=2] {'win'}, use_global_device_ids=true, to_apply=%region_0.0 | all-reduce | flops 8192 | bytes 65536 | tf_op jit(solution)/shard_map/psum | solution.py:19
  38.1 0.0 copy-done.3
  38.1 0.0 copy-done.2
  38.1 0.0 copy-start
  38.1 0.0 copy-start.1
  38.1 2.9 %fusion.7 = f32[8,8,16,128]{3,1,2,0:T(8,128)S(1)} fusion(bf16[8,16,128,128]{3,2,1,0:T(8,128)(2,1)} %param.8, f32[8,8,128]{2,1,0:T(8,128)S(1)} %psum.7, f32[8,128]{1,0:T(8,128)S(1)} %copy-done.2, f32[8,128]{1,0:T(8,128)S(1)} %copy-done.3), kind=kOutput, calls=%fused_computation.13 | convolution fusion | flops 33579008 | bytes 4759552 | tf_op jit(solution)/shard_map/bps,bksf->bkpf/dot_general | solution.py:21
  41.0 2.0 %scatter_custom_fusion = f32[256,1024]{1,0:T(8,128)S(1)} fusion(s32[128]{0:T(128)S(1)} %fusion.11, f32[16,8,8,128]{3,2,1,0:T(8,128)S(1)} %bitcast.34, f32[]{:T(128)} %constant.0.clone.1), kind=kCustom, calls=%fused_computation.3 | custom fusion | flops 131072 | bytes 1572868 | tf_op jit(solution)/shard_map/scatter-add | solution.py:25
  43.0 1.2 %copy.10 = f32[32,8,8,128]{3,2,1,0:T(8,128)} copy(f32[32,8,8,128]{3,1,2,0:T(8,128)S(1)} %bitcast.33) | data formatting | bytes 2097152
  44.2 0.0 reduce-scatter.2.cloned.1.call-update
  44.2 28.1 %reduce-scatter.2.cloned.1.call-done = f32[64,8,128]{2,1,0:T(8,128)} async-done(((f32[256,8,128]{2,1,0:T(8,128)}), f32[64,8,128]{2,1,0:T(8,128)}) %reduce-scatter.2.cloned.1.call-update) | async-done | bytes 262160 | tf_op jit(solution)/shard_map/reduce_scatter | solution.py:27
  72.3 0.0 copy-done
  72.3 0.0 copy-done.1
  72.3 1.7 %fusion.5 = f32[1,64,8,128]{3,2,1,0:T(8,128)} fusion(f32[64,8,128]{2,1,0:T(8,128)} %reduce-scatter.2.cloned.1.call-done, f32[1,64,8,128]{3,2,1,0:T(8,128)S(1)} %copy-done, f32[64,128]{1,0:T(8,128)S(1)} %bitcast.36), kind=kLoop, calls=%fused_computation.10 | loop fusion | flops 131072 | bytes 819200 | tf_op jit(solution)/shard_map/broadcast_in_dim | solution.py:34
  (2 shorter events, 0.0 us)
Async XLA Ops:
  6.5 31.6 %copy-start.3 = (f32[8,128]{1,0:T(8,128)S(1)}, f32[8,128]{1,0:T(8,128)}, u32[]{:S(2)}) copy-start(f32[8,128]{1,0:T(8,128)} %param.11) | copy-start | bytes 12292
  6.5 31.6 %copy-start.2 = (f32[8,128]{1,0:T(8,128)S(1)}, f32[8,128]{1,0:T(8,128)}, u32[]{:S(2)}) copy-start(f32[8,128]{1,0:T(8,128)} %param.10) | copy-start | bytes 12292
  6.5 65.8 %reduce-scatter.2.cloned.1.call-start = ((), (), s32[]{:S(2)}) async-start(), calls=%async_computation.1 | async-start | bytes 1310720 | tf_op jit(solution)/shard_map/reduce_scatter | solution.py:27
  38.1 34.2 %copy-start = (f32[1,64,8,128]{3,2,1,0:T(8,128)S(1)}, f32[1,64,8,128]{3,2,1,0:T(8,128)}, u32[]{:S(2)}) copy-start(f32[1,64,8,128]{3,2,1,0:T(8,128)} %param.6) | copy-start | bytes 786436
  38.1 34.2 %copy-start.1 = (f32[1,64,128]{2,1,0:T(8,128)S(1)}, f32[1,64,128]{2,1,0:T(8,128)}, u32[]{:S(2)}) copy-start(f32[1,64,128]{2,1,0:T(8,128)} %param.7) | copy-start | bytes 98308
Sparse Core Ops, SparseCore 0:
  44.3 27.9 reduce-scatter.1
where the time goes:
time: 81.1 us; the launch traced here: 80.9 us
  waiting for transfers between devices  28.2 us (35%)
  blocking collectives  25.7 us (32%)
  between operations  13.4 us (17%)
  matrix products  6.24 us (8%)
  other arithmetic  4.64 us (6%)
  local copies, waits for them, and re-layouts  2.68 us (3%)
    reduce_scatter x1, waiting for transfers between devices, body(): lax.psum_scatter(dense_terms.reshape(own_tiles * lax.axis_size('snd'), ha...  28.1 us
    all_gather x1, blocking collectives, body(): window_flux = lax.all_gather(rounded, 'snd', axis=0, tiled=True)  17.4 us
    psum x1, blocking collectives, body(): modeled = lax.psum(window_part, 'win')  8.35 us
    dot_general x1, matrix products, body(): jnp.einsum('bksf,bkpf->bps', footprint, gathered, preferred_element_type=...  3.36 us
    dot_general x1, matrix products, body(): jnp.einsum('bps,bksf->bkpf', residual, footprint, preferred_element_type=...  2.88 us
    scatter-add x1, other arithmetic, body(): jnp.zeros((window_tiles, half_points * tile_cells), jnp.float32)  1.96 us
    broadcast_in_dim x1, other arithmetic, body(): return gradient[None]  1.69 us
  transfers between devices with their start and end apart: 1, of which 1 were waited for; matrix products, arithmetic and copies ran while one was open for 0% of the time, Pallas kernels for 0%

commit v1 on v0

--- a/solution.py
+++ b/solution.py
@@ -16,7 +16,7 @@
     window_part = jnp.einsum(
         "bksf,bkpf->bps", footprint, gathered, preferred_element_type=jnp.float32
     )
-    modeled = lax.psum(window_part, "win")
+    modeled = jnp.sum(lax.all_gather(window_part, "win"), axis=0)
     residual = (obs_weight[:, None, :] * (modeled - observed[:, None, :])).astype(jnp.bfloat16)
     contrib = jnp.einsum("bps,bksf->bkpf", residual, footprint, preferred_element_type=jnp.float32)
     contrib = contrib.reshape(ref_count, half_points * tile_cells)

time: 81.1 us -> 78.3 us (0.965)
  blocking collectives: 25.7 us -> 22 us
  waiting for transfers between devices: 28.2 us -> 29.1 us
    psum x1 -> x0, blocking collectives: 8.35 us -> none  [body(): modeled = lax.psum(window_part, 'win')]
    all_gather x0 -> x1, blocking collectives: none -> 4.6 us  [body(): modeled = jnp.sum(lax.all_gather(window_part, 'win'), axis=0)]
    reduce_scatter x1, waiting for transfers between devices: 28.1 us -> 29.1 us  [body(): lax.psum_scatter(dense_terms.reshape(own_tiles * lax.axis_size('snd'), ha...]
where the time goes in v1:
time: 78.3 us; the launch traced here: 78 us
  waiting for transfers between devices  29.1 us (37%)
  blocking collectives  22 us (28%)
  between operations  13.4 us (17%)
  matrix products  6.24 us (8%)
  other arithmetic  4.64 us (6%)
  local copies, waits for them, and re-layouts  2.68 us (3%)
    reduce_scatter x1, waiting for transfers between devices, body(): lax.psum_scatter(dense_terms.reshape(own_tiles * lax.axis_size('snd'), ha...  29.1 us
    all_gather x1, blocking collectives, body(): window_flux = lax.all_gather(rounded, 'snd', axis=0, tiled=True)  17.4 us
    all_gather x1, blocking collectives, body(): modeled = jnp.sum(lax.all_gather(window_part, 'win'), axis=0)  4.6 us
    dot_general x1, matrix products, body(): jnp.einsum('bksf,bkpf->bps', footprint, gathered, preferred_element_type=...  3.36 us
    dot_general x1, matrix products, body(): jnp.einsum('bps,bksf->bkpf', residual, footprint, preferred_element_type=...  2.88 us
    scatter-add x1, other arithmetic, body(): jnp.zeros((window_tiles, half_points * tile_cells), jnp.float32)  1.96 us
    broadcast_in_dim x1, other arithmetic, body(): return gradient[None]  1.69 us
  transfers between devices with their start and end apart: 1, of which 1 were waited for; matrix products, arithmetic and copies ran while one was open for 0% of the time, Pallas kernels for 0%

profile of v1, /device:TPU:0, one launch (start us, length us, event | category | flops | bytes accessed | tf_op | source)
XLA Modules:
  0.0 78.0 jit_solution(15857444935830439632)
XLA Ops:
  6.5 0.0 copy-start.3
  6.5 0.0 copy-start.2
  6.5 0.0 reduce-scatter.2.cloned.1.call-start
  6.5 0.8 %reshape.43 = s32[128,1]{0,1:T(1,128)S(1)} reshape(s32[8,16]{1,0:T(8,128)} %param.9) | data formatting | bytes 1024 | tf_op jit(solution)/shard_map/reshape | solution.py:12
  7.3 1.0 %bitcast_convert_fusion = bf16[64,8,128]{2,1,0:T(8,128)(2,1)S(1)} fusion(f32[1,64,8,128]{3,2,1,0:T(8,128)} %param.6), kind=kLoop, calls=%fused_computation.8 | loop fusion | flops 65536 | bytes 393216 | tf_op jit(solution)/shard_map/convert_element_type | solution.py:13
  8.3 17.4 %all_gather.9 = bf16[256,8,128]{2,1,0:T(8,128)(2,1)S(1)} all-gather(bf16[64,8,128]{2,1,0:T(8,128)(2,1)S(1)} %bitcast_convert_fusion), channel_id=1, replica_groups=mesh['groups'=2,'snd'=4,'win'=2,'pt'=2] {'snd'}, dimensions={0}, use_global_device_ids=true | all-gather | bytes 655360 | tf_op jit(solution)/shard_map/all_gather | solution.py:14
  25.7 0.7 gather_fusion
  26.4 3.4 %convolution_bitcast_fusion = f32[8,8,128]{2,1,0:T(8,128)S(1)} fusion(bf16[8,16,8,128]{3,2,1,0:T(8,128)(2,1)S(1)} %bitcast.36, bf16[8,16,128,128]{3,2,1,0:T(8,128)(2,1)} %param.8), kind=kOutput, calls=%fused_computation.2 | convolution fusion | flops 33554432 | bytes 4489216 | tf_op jit(solution)/shard_map/bksf,bkpf->bps/dot_general | solution.py:16
  29.7 4.6 %all-gather = f32[16,8,128]{2,1,0:T(8,128)S(1)} all-gather(f32[8,8,128]{2,1,0:T(8,128)S(1)} %convolution_bitcast_fusion), channel_id=2, replica_groups=mesh['groups'=2,'snd'=4,'win'=2,'pt'=2] {'win'}, dimensions={0}, use_global_device_ids=true | all-gather | bytes 98304 | tf_op jit(solution)/shard_map/all_gather | solution.py:19
  34.3 0.0 copy-done.3
  34.3 0.0 copy-done.2
  34.3 0.0 copy-start
  34.4 0.0 copy-start.1
  34.4 2.9 %fusion.7 = f32[8,8,16,128]{3,1,2,0:T(8,128)S(1)} fusion(bf16[8,16,128,128]{3,2,1,0:T(8,128)(2,1)} %param.8, f32[8,8,128]{2,1,0:T(8,128)S(1)} %reduce_sum.9, f32[8,128]{1,0:T(8,128)S(1)} %copy-done.2, f32[8,128]{1,0:T(8,128)S(1)} %copy-done.3), kind=kOutput, calls=%fused_computation.13 | convolution fusion | flops 33579008 | bytes 4759552 | tf_op jit(solution)/shard_map/bps,bksf->bkpf/dot_general | solution.py:21
  37.3 2.0 %scatter_custom_fusion = f32[256,1024]{1,0:T(8,128)S(1)} fusion(s32[128]{0:T(128)S(1)} %fusion.11, f32[16,8,8,128]{3,2,1,0:T(8,128)S(1)} %bitcast.35, f32[]{:T(128)} %constant.3.clone.1), kind=kCustom, calls=%fused_computation.3 | custom fusion | flops 131072 | bytes 1572868 | tf_op jit(solution)/shard_map/scatter-add | solution.py:25
  39.2 1.2 %copy.10 = f32[32,8,8,128]{3,2,1,0:T(8,128)} copy(f32[32,8,8,128]{3,1,2,0:T(8,128)S(1)} %bitcast.34) | data formatting | bytes 2097152
  40.4 0.0 reduce-scatter.2.cloned.1.call-update
  40.4 29.1 %reduce-scatter.2.cloned.1.call-done = f32[64,8,128]{2,1,0:T(8,128)} async-done(((f32[256,8,128]{2,1,0:T(8,128)}), f32[64,8,128]{2,1,0:T(8,128)}) %reduce-scatter.2.cloned.1.call-update) | async-done | bytes 262160 | tf_op jit(solution)/shard_map/reduce_scatter | solution.py:27
  69.5 0.0 copy-done
  69.5 0.0 copy-done.1
  69.5 1.7 %fusion.5 = f32[1,64,8,128]{3,2,1,0:T(8,128)} fusion(f32[64,8,128]{2,1,0:T(8,128)} %reduce-scatter.2.cloned.1.call-done, f32[1,64,8,128]{3,2,1,0:T(8,128)S(1)} %copy-done, f32[64,128]{1,0:T(8,128)S(1)} %bitcast.38), kind=kLoop, calls=%fused_computation.10 | loop fusion | flops 131072 | bytes 819200 | tf_op jit(solution)/shard_map/broadcast_in_dim | solution.py:34
  (3 shorter events, 0.0 us)
Async XLA Ops:
  6.5 27.8 %copy-start.3 = (f32[8,128]{1,0:T(8,128)S(1)}, f32[8,128]{1,0:T(8,128)}, u32[]{:S(2)}) copy-start(f32[8,128]{1,0:T(8,128)} %param.11) | copy-start | bytes 12292
  6.5 27.8 %copy-start.2 = (f32[8,128]{1,0:T(8,128)S(1)}, f32[8,128]{1,0:T(8,128)}, u32[]{:S(2)}) copy-start(f32[8,128]{1,0:T(8,128)} %param.10) | copy-start | bytes 12292
  6.5 63.0 %reduce-scatter.2.cloned.1.call-start = ((), (), s32[]{:S(2)}) async-start(), calls=%async_computation.1 | async-start | bytes 1310720 | tf_op jit(solution)/shard_map/reduce_scatter | solution.py:27
  34.3 35.2 %copy-start = (f32[1,64,8,128]{3,2,1,0:T(8,128)S(1)}, f32[1,64,8,128]{3,2,1,0:T(8,128)}, u32[]{:S(2)}) copy-start(f32[1,64,8,128]{3,2,1,0:T(8,128)} %param.6) | copy-start | bytes 786436
  34.4 35.1 %copy-start.1 = (f32[1,64,128]{2,1,0:T(8,128)S(1)}, f32[1,64,128]{2,1,0:T(8,128)}, u32[]{:S(2)}) copy-start(f32[1,64,128]{2,1,0:T(8,128)} %param.7) | copy-start | bytes 98308
Sparse Core Ops, SparseCore 0:
  40.6 28.8 reduce-scatter.1
